TPU v7x, 512 devices: a whole 4x8x8 slice. The times are simulated.
512 devices in a mesh: section: 2 (over core), sy: 8 (over y), sx: 8 (over z), mb: 4 (over x).
Axes of the slice: x: 4, y: 8, z: 8, core: 2. Of those that a mesh axis runs over, the one named last changes fastest.
Arguments:
- frames: bfloat16 [4, 512, 512, 128], P('mb', 'sy', 'sx'), may hold values from -6 to 6
- encode_weight: bfloat16 [512, 384], replicated, may hold values from -0.25 to 0.25
- conv_weight: bfloat16 [2, 1, 3456, 384], P('section', None, ('sy', 'sx')), may hold values from -0.109375 to 0.109375
- norm_gain: float32 [2, 1, 384], P('section'), may hold values from 0.1 to 1.9
- head_weight: bfloat16 [384, 256], replicated, may hold values from -0.3125 to 0.3125
- prior_logits: bfloat16 [4, 256, 256, 256], P('mb', 'sy', 'sx'), may hold values from -12 to 249
- target_bins: int32 [4, 256, 256], P('mb', 'sy', 'sx'), may hold values from 0 to 255
Outputs:
- section_features: bfloat16 [2, 4, 256, 256, 384], P('section', 'mb', 'sy', 'sx')
- head_step: float32 [384, 256], P('section')
- mean_loss: float32 [], replicated
All inputs are finite; a program needn't handle non-finite values.
Results may differ from a plain program's by a relative error of at most 0.008.
Values may be sent and summed in bfloat16 or wider, within the bound.
No kernel may reach another device: no remote copies, remote signals or barrier semaphores. Data moves between devices by JAX's collectives and lax.ppermute only.
A program may use at most 64 MiB of HBM per device.

v0:
```python
import jax
import jax.numpy as jnp
from jax import lax
from jax.sharding import PartitionSpec as P

FIRST_DILATION = 1


def padded_2(block, sides, width):
    for axis, dim in sides:
        count = lax.axis_size(axis)
        forward = [(i, i + 1) for i in range(count - 1)]
        backward = [(target, source) for source, target in forward]
        low = lax.ppermute(
            lax.slice_in_dim(block, block.shape[dim] - width, None, axis=dim), axis, forward
        )
        high = lax.ppermute(lax.slice_in_dim(block, 0, width, axis=dim), axis, backward)
        block = jnp.concatenate([low, block, high], axis=dim)
    return block


def from_behind(block, axis, distance):
    devices = range(lax.axis_size(axis))
    route = [(i - distance, i) for i in devices if i - distance in devices]
    return lax.ppermute(block, axis, route)


def norm_gelu(activations, gain):
    values = activations.astype(jnp.float32)
    center = jnp.mean(values, axis=-1, keepdims=True)
    offset = values - center
    spread = jnp.mean(offset * offset, axis=-1, keepdims=True)
    normed = offset * lax.rsqrt(spread + 1e-05) * gain
    return jax.nn.gelu(normed, approximate=False).astype(jnp.bfloat16)


def per_device(
    frames, encode_weight, conv_weight, norm_gain, head_weight, prior_logits, target_bins
):
    first_section = lax.axis_index("section") == 0
    micro_count = frames.shape[0]
    side_cells = frames.shape[1] // 2
    input_width = frames.shape[3]
    channels = encode_weight.shape[1]
    bins_count = head_weight.shape[1]
    parts_y = lax.axis_size("sy")
    parts_x = lax.axis_size("sx")
    cell_count = side_cells * side_cells
    kernel = encode_weight.reshape(2, 2, input_width, channels)
    grad_total = jnp.zeros((channels, bins_count), jnp.float32)
    loss_total = jnp.zeros((), jnp.float32)
    first_out = []
    second_out = []
    handed = None
    for tick_index in range(micro_count + 1):
        if tick_index == 0:
            blocks = frames[0].reshape(side_cells, 2, side_cells, 2, input_width)
            activations = jnp.einsum(
                "apbqc,pqco->abo", blocks, kernel, preferred_element_type=jnp.float32
            ).astype(jnp.bfloat16)
        else:
            activations = handed
        apply_reach = FIRST_DILATION * 2**0
        hidden = norm_gelu(activations, norm_gain[0, 0])
        haloed = padded_2(hidden, (("sy", 0), ("sx", 1)), apply_reach)
        zero_padded = jnp.pad(
            hidden, ((apply_reach, apply_reach), (apply_reach, apply_reach), (0, 0))
        )
        apply_padded = jnp.where(first_section, haloed, zero_padded)
        windows = [
            apply_padded[
                tap_row * apply_reach : tap_row * apply_reach + side_cells,
                tap_column * apply_reach : tap_column * apply_reach + side_cells,
            ]
            for tap_row in range(3)
            for tap_column in range(3)
        ]
        patches = jnp.concatenate(windows, axis=2).reshape(cell_count, 9 * channels)
        summed = jnp.dot(
            patches,
            lax.all_gather(conv_weight[0, 0], ("sy", "sx"), axis=0, tiled=True),
            preferred_element_type=jnp.float32,
        )
        activations = (
            activations.astype(jnp.float32) + summed.reshape(side_cells, side_cells, channels)
        ).astype(jnp.bfloat16)
        if tick_index < micro_count:
            first_out.append(activations)
        rows_y = side_cells // parts_y
        rows_x = side_cells // parts_x
        plain_view = activations.reshape(parts_y, rows_y, parts_x, rows_x, channels)
        spaced = activations.reshape(rows_y, parts_y, rows_x, parts_x, channels).transpose(
            1, 0, 3, 2, 4
        )
        outgoing = jnp.where(first_section, spaced, plain_view)
        arrived = lax.all_to_all(
            lax.all_to_all(outgoing, "sy", split_axis=0, concat_axis=0, tiled=True),
            "sx",
            split_axis=2,
            concat_axis=2,
            tiled=True,
        )
        direct = arrived.reshape(side_cells, side_cells, channels)
        restored = arrived.transpose(1, 0, 3, 2, 4).reshape(side_cells, side_cells, channels)
        moved = jnp.where(first_section, direct, restored)
        if tick_index >= 1:
            second_out.append(moved)
            flat_rows = moved.reshape(cell_count, channels)
            logits = jnp.dot(flat_rows, head_weight, preferred_element_type=jnp.float32)
            logits = logits + prior_logits[tick_index - 1].reshape(cell_count, bins_count).astype(
                jnp.float32
            )
            row_top = jnp.max(logits, axis=1, keepdims=True)
            shifted = logits - row_top
            exp_terms = jnp.exp(shifted)
            exp_total = jnp.sum(exp_terms, axis=1, keepdims=True)
            softmax_rows = exp_terms / exp_total
            onehot = (
                target_bins[tick_index - 1].reshape(cell_count, 1)
                == lax.broadcasted_iota(jnp.int32, (1, bins_count), 1)
            ).astype(jnp.float32)
            loss_sum = jnp.sum(jnp.log(exp_total[:, 0]) - jnp.sum(shifted * onehot, axis=1))
            delta_rows = (softmax_rows - onehot).astype(jnp.bfloat16)
            grad_part = lax.dot_general(
                flat_rows, delta_rows, (((0,), (0,)), ((), ())), preferred_element_type=jnp.float32
            )
            grad_part, loss_sum = (grad_part, loss_sum)
            grad_total = jnp.where(first_section, 0.0, grad_part)
            loss_total = jnp.where(first_section, 0.0, loss_sum)
        if tick_index < micro_count:
            handed = from_behind(moved, "section", 1)
    stacked = jnp.stack([jnp.where(first_section, first_out[0], second_out[0])])[None]
    gradient, loss_all = lax.psum((grad_total, loss_total), ("sy", "sx", "mb"))
    head_full = gradient * lax.rsqrt(jnp.mean(gradient * gradient) + 1e-06)
    mean_local = loss_all / (micro_count * lax.axis_size("mb") * cell_count * parts_y * parts_x)
    half_rows = channels // 2
    sent_rows, sent_loss = (
        from_behind(head_full[:half_rows].astype(jnp.bfloat16), "section", -1).astype(jnp.float32),
        from_behind(mean_local.astype(jnp.bfloat16), "section", -1).astype(mean_local.dtype),
    )
    head_step = jnp.where(first_section, sent_rows, head_full[half_rows:])
    mean_loss = jnp.where(first_section, sent_loss, mean_local)
    return (stacked, head_step, mean_loss)


def solution(mesh):
    placed = (
        P("mb", "sy", "sx", None),
        P(),
        P("section", None, ("sy", "sx"), None),
        P("section", None, None),
        P(),
        P("mb", "sy", "sx", None),
        P("mb", "sy", "sx"),
    )
    return jax.shard_map(
        per_device,
        mesh=mesh,
        in_specs=placed,
        out_specs=(P("section", "mb", "sy", "sx", None), P("section", None), P()),
        check_vma=False,
    )
```

profile of v0, /device:TPU:1, one launch (start us, length us, event | category | flops | bytes accessed | tf_op | source)
XLA Modules:
  0.0 957.4 jit_solution(2720262242174057233)
XLA Ops:
  7.2 1.5 copy.50
  9.5 2.0 convert_reduce_fusion.1
  12.0 3.8 fusion.20
  15.9 4.0 collective-permute-start
  19.9 1.3 collective-permute-start.1
  21.2 3.3 collective-permute-done.1
  24.6 4.0 collective-permute-start.2
  29.9 4.2 collective-permute-done.3
  37.0 1.3 slice_dynamic-update-slice_fusion.15
  42.9 1.4 slice_dynamic-update-slice_fusion.10
  45.5 57.8 %all-gather.3.cloned.1.call-done = bf16[1,1,3456,384]{3,1,0,2:T(2,128)(2,1)} async-done(((bf16[1,1,54,384]{3,1,0,2:T(2,128)(2,1)}), bf16[1,1,3456,384]{3,1,0,2:T(2,128)(2,1)}) %all-gather.3.cloned.1.call-update) | async-done | bytes 2654224 | tf_op jit(solution)/shard_map/all_gather | solution.py:81
  103.3 8.4 fusion.22
  112.4 23.7 %all_to_all.20 = bf16[8,4,8,4,384]{4,3,1,2,0:T(4,128)(2,1)S(1)} all-to-all(bf16[8,4,8,4,384]{4,3,1,2,0:T(4,128)(2,1)S(1)} %bitcast_select_fusion.2), channel_id=1, replica_groups=mesh['section'=2,'sy'=8,'sx'=8,'mb'=4] {'sy'}, dimensions={0} | all-to-all | bytes 1572864 | tf_op jit(solution)/shard_map/all_to_all | solution.py:97
  136.3 19.7 %all_to_all.21 = bf16[8,4,8,4,384]{4,3,1,0,2:T(4,128)(2,1)S(1)} all-to-all(bf16[8,4,8,4,384]{4,3,1,0,2:T(4,128)(2,1)S(1)} %copy.53), channel_id=1, replica_groups=mesh['section'=2,'sy'=8,'sx'=8,'mb'=4] {'sx'}, dimensions={2} | all-to-all | bytes 1572864 | tf_op jit(solution)/shard_map/all_to_all | solution.py:96
  157.3 1.5 collective-permute-start.4
  158.8 9.2 collective-permute-done.4
  168.8 3.8 fusion.13
  172.6 1.4 collective-permute-start.5
  174.0 1.3 collective-permute-start.6
  175.3 3.3 collective-permute-done.6
  178.7 2.2 collective-permute-start.7
  182.2 3.6 collective-permute-done.8
  189.1 3.9 fusion.24
  193.6 24.2 %all_to_all.22 = bf16[8,4,8,4,384]{4,3,1,2,0:T(4,128)(2,1)S(1)} all-to-all(bf16[8,4,8,4,384]{4,3,1,2,0:T(4,128)(2,1)S(1)} %bitcast_select_fusion.1), channel_id=1, replica_groups=mesh['section'=2,'sy'=8,'sx'=8,'mb'=4] {'sy'}, dimensions={0} | all-to-all | bytes 1572864 | tf_op jit(solution)/shard_map/all_to_all | solution.py:97
  219.0 3.5 all-to-all-start.3
  222.9 1.3 copy.63
  225.1 16.5 %all-to-all-done.3 = bf16[8,4,8,4,384]{4,3,1,0,2:T(4,128)(2,1)S(1)} async-done(((bf16[8,4,8,4,384]{4,3,1,0,2:T(4,128)(2,1)}), bf16[8,4,8,4,384]{4,3,1,0,2:T(4,128)(2,1)S(1)}, u32[]{:S(2)}, u32[]{:S(2)}) %all-to-all-start.3) | async-done | bytes 786464 | tf_op jit(solution)/shard_map/all_to_all | solution.py:96
  246.1 1.3 convolution_select_fusion
  248.7 575.3 %psum.15 = f32[]{:T(128)} all-reduce(f32[]{:T(128)S(6)} %select_n.85), channel_id=1, replica_groups=mesh['section'=2,'sy'=8,'sx'=8,'mb'=4] {'sy','sx','mb'}, use_global_device_ids=true, to_apply=%region_10.11 | all-reduce | flops 1 | bytes 8 | tf_op jit(solution)/shard_map/psum | solution.py:133
  824.8 117.5 %collective-permute-start.10 = (bf16[]{:T(256)}, bf16[]{:T(256)}, u32[]{:S(2)}, u32[]{:S(2)}) collective-permute-start(bf16[]{:T(256)} %convert_element_type.60), channel_id=1, source_target_pairs={{256,0},{257,1},{258,2},{259,3},{260,4},{261,5},{262,6},{263,7},{2... | collective-permute-start | bytes 14 | tf_op jit(solution)/shard_map/ppermute | solution.py:25
  942.3 1.7 multiply_reduce_fusion
  945.7 1.3 collective-permute-start.9
  (82 shorter events, 30.0 us)
Async XLA Ops:
  7.2 2.3 copy-start
  7.2 96.1 %all-gather.3.cloned.1.call-start = ((), (), s32[]{:S(2)}) async-start(), calls=%async_computation.5 | async-start | bytes 5391360 | tf_op jit(solution)/shard_map/all_gather | solution.py:81
  15.9 5.3 collective-permute-start
  19.9 4.6 collective-permute-start.1
  24.6 5.3 collective-permute-start.2
  28.6 5.5 collective-permute-start.3
  157.3 10.7 %collective-permute-start.4 = (bf16[32,32,384]{2,1,0:T(8,128)(2,1)S(1)}, bf16[32,32,384]{2,1,0:T(8,128)(2,1)S(1)}, u32[]{:S(2)}, u32[]{:S(2)}) collective-permute-start(bf16[32,32,384]{2,1,0:T(8,128)(2,1)S(1)} %broadcast_select_fusion), channel_id=1, source_target_pairs={{0,256},{1,257},{2,258},{3,259},{4,260},{5,261},{6,262},{7,263},{8... | collective-permute-start | bytes 2359304 | tf_op jit(solution)/shard_map/ppermute | solution.py:25
  172.6 2.7 collective-permute-start.5
  174.0 4.6 collective-permute-start.6
  178.7 3.5 collective-permute-start.7
  180.9 4.9 collective-permute-start.8
  186.3 2.8 slice-start
  187.4 1.7 slice-start.1
  217.8 5.0 copy-start.3
  219.0 22.6 %all-to-all-start.3 = ((bf16[8,4,8,4,384]{4,3,1,0,2:T(4,128)(2,1)}), bf16[8,4,8,4,384]{4,3,1,0,2:T(4,128)(2,1)S(1)}, u32[]{:S(2)}, u32[]{:S(2)}) async-start(bf16[8,4,8,4,384]{4,3,1,0,2:T(4,128)(2,1)} %copy.58), calls=%async_computation.3 | async-start | bytes 1572864 | tf_op jit(solution)/shard_map/all_to_all | solution.py:96
  222.5 719.8 %all-reduce.4.cloned.1.call-start = ((), (), s32[]{:S(2)}) async-start(), calls=%async_computation.4 | async-start | bytes 786432 | tf_op jit(solution)/shard_map/psum | solution.py:133
  243.0 1.1 copy-start.2
  244.1 1.2 copy-start.1
  244.1 1.2 copy-start.4
  824.8 123.2 %collective-permute-start.10 = (bf16[]{:T(256)}, bf16[]{:T(256)}, u32[]{:S(2)}, u32[]{:S(2)}) collective-permute-start(bf16[]{:T(256)} %convert_element_type.60), channel_id=1, source_target_pairs={{256,0},{257,1},{258,2},{259,3},{260,4},{261,5},{262,6},{263,7},{2... | collective-permute-start | bytes 14 | tf_op jit(solution)/shard_map/ppermute | solution.py:25
  945.7 2.9 collective-permute-start.9
Sparse Core Ops, SparseCore 0:
  11.7 91.6 all-gather.2
  247.5 225.9 all-reduce.3
where the time goes:
time: 958 us; the launch traced here: 957 us
  blocking collectives  643 us (67%)
  starting transfers between devices  141 us (15%)
  waiting for transfers between devices  97.9 us (10%)
  local copies, waits for them, and re-layouts  24 us (3%)
  between operations  18.2 us (2%)
  other arithmetic  17.5 us (2%)
  matrix products  16.1 us (2%)
    psum x1, blocking collectives, per_device(): gradient, loss_all = lax.psum((grad_total, loss_total), ('sy', 'sx', 'mb'))  575 us
    ppermute x3, starting transfers between devices, from_behind(): return lax.ppermute(block, axis, route)  120 us
    all_gather x1, waiting for transfers between devices, per_device(): lax.all_gather(conv_weight[0, 0], ('sy', 'sx'), axis=0, tiled=True)  57.8 us
    all_to_all x2, blocking collectives, per_device(): lax.all_to_all(outgoing, 'sy', split_axis=0, concat_axis=0, tiled=True)  47.8 us
    all_to_all x1, blocking collectives, per_device(): lax.all_to_all(lax.all_to_all(outgoing, 'sy', split_axis=0, concat_axis=0...  19.7 us
  transfers between devices with their start and end apart: 14, of which 7 were waited for; matrix products, arithmetic and copies ran while one was open for 3% of the time, Pallas kernels for 0%

commit v1 on v0

--- a/solution.py
+++ b/solution.py
@@ -4,6 +4,11 @@
 from jax.sharding import PartitionSpec as P
 
 FIRST_DILATION = 1
+
+
+def axis_by_axis(x, axis_one, axis_two):
+    partial = lax.psum(x, axis_one)
+    return lax.psum(partial, axis_two)
 
 
 def padded_2(block, sides, width):
@@ -130,7 +135,7 @@
         if tick_index < micro_count:
             handed = from_behind(moved, "section", 1)
     stacked = jnp.stack([jnp.where(first_section, first_out[0], second_out[0])])[None]
-    gradient, loss_all = lax.psum((grad_total, loss_total), ("sy", "sx", "mb"))
+    gradient, loss_all = axis_by_axis((grad_total, loss_total), ("sx", "mb"), "sy")
     head_full = gradient * lax.rsqrt(jnp.mean(gradient * gradient) + 1e-06)
     mean_local = loss_all / (micro_count * lax.axis_size("mb") * cell_count * parts_y * parts_x)
     half_rows = channels // 2

time: 958 us -> 514 us (0.54)
  blocking collectives: 643 us -> 141 us
  waiting for transfers between devices: 97.9 us -> 247 us
  starting transfers between devices: 141 us -> 48.3 us
    psum x1 -> x2, blocking collectives: 575 us -> 73.4 us  [the longest x1 58.8 us: axis_by_axis(): partial = lax.psum(x, axis_one)]
    psum x1 -> x2, waiting for transfers between devices: 0.01 us -> 150 us  [the longest x1 150 us: axis_by_axis(): partial = lax.psum(x, axis_one)]
    ppermute x3, starting transfers between devices: 120 us -> 27.7 us  [from_behind(): return lax.ppermute(block, axis, route)]
  transfers between devices with their start and end apart: 14 -> 15, of which waited for: 7 -> 8; matrix products, arithmetic and copies ran while one was open for 3% -> 5% of each run, Pallas kernels for 0% -> 0%
where the time goes in v1:
time: 514 us; the launch traced here: 513 us
  waiting for transfers between devices  247 us (48%)
  blocking collectives  141 us (27%)
  starting transfers between devices  48.3 us (9%)
  local copies, waits for them, and re-layouts  24.6 us (5%)
  other arithmetic  18.4 us (4%)
  between operations  18 us (4%)
  matrix products  16 us (3%)
    psum x1, waiting for transfers between devices, axis_by_axis(): partial = lax.psum(x, axis_one)  150 us
    psum x1, blocking collectives, axis_by_axis(): partial = lax.psum(x, axis_one)  58.8 us
    all_gather x1, waiting for transfers between devices, per_device(): lax.all_gather(conv_weight[0, 0], ('sy', 'sx'), axis=0, tiled=True)  57.8 us
    all_to_all x2, blocking collectives, per_device(): lax.all_to_all(outgoing, 'sy', split_axis=0, concat_axis=0, tiled=True)  47.8 us
    ppermute x3, starting transfers between devices, from_behind(): return lax.ppermute(block, axis, route)  27.7 us
    all_to_all x1, blocking collectives, per_device(): lax.all_to_all(lax.all_to_all(outgoing, 'sy', split_axis=0, concat_axis=0...  19.7 us
    all_to_all x1, waiting for transfers between devices, per_device(): lax.all_to_all(lax.all_to_all(outgoing, 'sy', split_axis=0, concat_axis=0...  15 us
    unnamed x33, local copies, waits for them, and re-layouts  15 us
  transfers between devices with their start and end apart: 15, of which 8 were waited for; matrix products, arithmetic and copies ran while one was open for 5% of the time, Pallas kernels for 0%

profile of v1, /device:TPU:1, one launch (start us, length us, event | category | flops | bytes accessed | tf_op | source)
XLA Modules:
  0.0 513.0 jit_solution(13120472401288651312)
XLA Ops:
  7.2 1.5 copy.50
  9.5 2.0 convert_reduce_fusion.1
  12.0 3.8 fusion.20
  15.8 4.0 collective-permute-start
  21.2 3.3 collective-permute-done.1
  24.5 4.0 collective-permute-start.2
  29.9 4.2 collective-permute-done.3
  37.0 1.3 slice_dynamic-update-slice_fusion.15
  42.9 1.4 slice_dynamic-update-slice_fusion.10
  45.5 57.8 %all-gather.3.cloned.1.call-done = bf16[1,1,3456,384]{3,1,0,2:T(2,128)(2,1)} async-done(((bf16[1,1,54,384]{3,1,0,2:T(2,128)(2,1)}), bf16[1,1,3456,384]{3,1,0,2:T(2,128)(2,1)}) %all-gather.3.cloned.1.call-update) | async-done | bytes 2654224 | tf_op jit(solution)/shard_map/all_gather | solution.py:86
  103.3 8.4 %fusion.22 = bf16[32,32,384]{2,1,0:T(8,128)(2,1)S(1)} fusion(bf16[32,32,384]{2,1,0:T(8,128)(2,1)S(1)} %get-tuple-element.14, bf16[32,32,3456]{2,1,0:T(8,128)(2,1)} %slice_dynamic-update-slice_fusion.9, bf16[1,1,3456,384]{3,1,0,2:T(2,128)(2,1)} %all-gather.3.cloned.1.call-done), kind=kOutput, calls=%fused_computation.30 | convolution fusion | flops 2719088640 | bytes 11304960 | tf_op jit(solution)/shard_map/dot_general | solution.py:84
  112.3 23.7 %all_to_all.20 = bf16[8,4,8,4,384]{4,3,1,2,0:T(4,128)(2,1)S(1)} all-to-all(bf16[8,4,8,4,384]{4,3,1,2,0:T(4,128)(2,1)S(1)} %bitcast_select_fusion.2), channel_id=1, replica_groups=mesh['section'=2,'sy'=8,'sx'=8,'mb'=4] {'sy'}, dimensions={0} | all-to-all | bytes 1572864 | tf_op jit(solution)/shard_map/all_to_all | solution.py:102
  136.3 19.7 %all_to_all.21 = bf16[8,4,8,4,384]{4,3,1,0,2:T(4,128)(2,1)S(1)} all-to-all(bf16[8,4,8,4,384]{4,3,1,0,2:T(4,128)(2,1)S(1)} %copy.53), channel_id=1, replica_groups=mesh['section'=2,'sy'=8,'sx'=8,'mb'=4] {'sx'}, dimensions={2} | all-to-all | bytes 1572864 | tf_op jit(solution)/shard_map/all_to_all | solution.py:101
  157.3 1.5 collective-permute-start.4
  158.8 9.2 %collective-permute-done.4 = bf16[32,32,384]{2,1,0:T(8,128)(2,1)S(1)} collective-permute-done((bf16[32,32,384]{2,1,0:T(8,128)(2,1)S(1)}, bf16[32,32,384]{2,1,0:T(8,128)(2,1)S(1)}, u32[]{:S(2)}, u32[]{:S(2)}) %collective-permute-start.4) | collective-permute-done | bytes 786464 | tf_op jit(solution)/shard_map/ppermute | solution.py:30
  168.7 3.8 fusion.13
  172.6 1.4 collective-permute-start.5
  175.3 3.3 collective-permute-done.6
  178.6 2.2 collective-permute-start.7
  182.1 3.6 collective-permute-done.8
  189.1 3.9 fusion.24
  193.6 24.2 %all_to_all.22 = bf16[8,4,8,4,384]{4,3,1,2,0:T(4,128)(2,1)S(1)} all-to-all(bf16[8,4,8,4,384]{4,3,1,2,0:T(4,128)(2,1)S(1)} %bitcast_select_fusion.1), channel_id=1, replica_groups=mesh['section'=2,'sy'=8,'sx'=8,'mb'=4] {'sy'}, dimensions={0} | all-to-all | bytes 1572864 | tf_op jit(solution)/shard_map/all_to_all | solution.py:102
  218.9 3.5 all-to-all-start.3
  223.9 2.6 copy.63
  226.5 15.0 %all-to-all-done.3 = bf16[8,4,8,4,384]{4,3,1,0,2:T(4,128)(2,1)S(1)} async-done(((bf16[8,4,8,4,384]{4,3,1,0,2:T(4,128)(2,1)}), bf16[8,4,8,4,384]{4,3,1,0,2:T(4,128)(2,1)S(1)}, u32[]{:S(2)}, u32[]{:S(2)}) %all-to-all-start.3) | async-done | bytes 786464 | tf_op jit(solution)/shard_map/all_to_all | solution.py:101
  246.0 1.3 convolution_select_fusion
  247.4 150.4 %all-reduce.5.cloned.1.call-done = f32[384,256]{1,0:T(8,128)} async-done(((f32[384,256]{1,0:T(8,128)}), f32[384,256]{1,0:T(8,128)}) %all-reduce.5.cloned.1.call-update) | async-done | bytes 393232 | tf_op jit(solution)/shard_map/psum | solution.py:10
  399.1 58.8 %psum.30 = f32[]{:T(128)} all-reduce(f32[]{:T(128)S(6)} %select_n.85), channel_id=1, replica_groups=mesh['section'=2,'sy'=8,'sx'=8,'mb'=4] {'sx','mb'}, use_global_device_ids=true, to_apply=%region_11.12 | all-reduce | flops 1 | bytes 8 | tf_op jit(solution)/shard_map/psum | solution.py:10
  457.9 14.6 %psum.31 = f32[]{:T(128)} all-reduce(f32[]{:T(128)} %psum.30), channel_id=1, replica_groups=mesh['section'=2,'sy'=8,'sx'=8,'mb'=4] {'sy'}, use_global_device_ids=true, to_apply=%region_12.13 | all-reduce | flops 1 | bytes 8 | tf_op jit(solution)/shard_map/psum | solution.py:11
  473.3 24.9 %collective-permute-start.10 = (bf16[]{:T(256)}, bf16[]{:T(256)}, u32[]{:S(2)}, u32[]{:S(2)}) collective-permute-start(bf16[]{:T(256)} %convert_element_type.60), channel_id=1, source_target_pairs={{256,0},{257,1},{258,2},{259,3},{260,4},{261,5},{262,6},{263,7},{2... | collective-permute-start | bytes 14 | tf_op jit(solution)/shard_map/ppermute | solution.py:30
  498.2 1.7 multiply_reduce_fusion
  501.7 1.3 collective-permute-start.9
  (88 shorter events, 32.9 us)
Async XLA Ops:
  7.2 2.3 copy-start
  7.2 96.1 %all-gather.3.cloned.1.call-start = ((), (), s32[]{:S(2)}) async-start(), calls=%async_computation.6 | async-start | bytes 5391360 | tf_op jit(solution)/shard_map/all_gather | solution.py:86
  15.8 5.3 %collective-permute-start = (bf16[1,32,384]{2,1,0:T(8,128)(2,1)S(1)}, bf16[1,32,384]{2,1,0:T(8,128)(2,1)S(1)}, u32[]{:S(2)}, u32[]{:S(2)}) collective-permute-start(bf16[1,32,384]{2,1,0:T(8,128)(2,1)S(1)} %get-tuple-element.11), channel_id=1, source_target_pairs={{0,32},{32,64},{64,96},{96,128},{128,160},{160,192},{192,224},{1,3... | collective-permute-start | bytes 73736 | tf_op jit(solution)/shard_map/ppermute | solution.py:19
  19.9 4.6 collective-permute-start.1
  24.5 5.3 %collective-permute-start.2 = (bf16[34,1,384]{2,1,0:T(2,128)(2,1)S(1)}, bf16[34,1,384]{2,1,0:T(2,128)(2,1)S(1)}, u32[]{:S(2)}, u32[]{:S(2)}) collective-permute-start(bf16[34,1,384]{2,1,0:T(2,128)(2,1)S(1)} %get-tuple-element.7), channel_id=1, source_target_pairs={{0,4},{4,8},{8,12},{12,16},{16,20},{20,24},{24,28},{1,5},{5,9},{9,... | collective-permute-start | bytes 78344 | tf_op jit(solution)/shard_map/ppermute | solution.py:19
  28.6 5.5 %collective-permute-start.3 = (bf16[34,1,384]{2,1,0:T(2,128)(2,1)S(1)}, bf16[34,1,384]{2,1,0:T(2,128)(2,1)S(1)}, u32[]{:S(2)}, u32[]{:S(2)}) collective-permute-start(bf16[34,1,384]{2,1,0:T(2,128)(2,1)S(1)} %get-tuple-element.8), channel_id=1, source_target_pairs={{4,0},{8,4},{12,8},{16,12},{20,16},{24,20},{28,24},{5,1},{9,5},{13... | collective-permute-start | bytes 78344 | tf_op jit(solution)/shard_map/ppermute | solution.py:22
  157.3 10.7 %collective-permute-start.4 = (bf16[32,32,384]{2,1,0:T(8,128)(2,1)S(1)}, bf16[32,32,384]{2,1,0:T(8,128)(2,1)S(1)}, u32[]{:S(2)}, u32[]{:S(2)}) collective-permute-start(bf16[32,32,384]{2,1,0:T(8,128)(2,1)S(1)} %broadcast_select_fusion), channel_id=1, source_target_pairs={{0,256},{1,257},{2,258},{3,259},{4,260},{5,261},{6,262},{7,263},{8... | collective-permute-start | bytes 2359304 | tf_op jit(solution)/shard_map/ppermute | solution.py:30
  172.6 2.7 collective-permute-start.5
  174.0 4.6 collective-permute-start.6
  178.6 3.5 collective-permute-start.7
  180.8 4.9 collective-permute-start.8
  186.3 2.8 slice-start
  187.3 1.7 slice-start.1
  217.7 5.0 copy-start.3
  218.9 22.6 %all-to-all-start.3 = ((bf16[8,4,8,4,384]{4,3,1,0,2:T(4,128)(2,1)}), bf16[8,4,8,4,384]{4,3,1,0,2:T(4,128)(2,1)S(1)}, u32[]{:S(2)}, u32[]{:S(2)}) async-start(bf16[8,4,8,4,384]{4,3,1,0,2:T(4,128)(2,1)} %copy.58), calls=%async_computation.3 | async-start | bytes 1572864 | tf_op jit(solution)/shard_map/all_to_all | solution.py:101
  222.5 4.0 copy-start.5
  222.5 175.3 %all-reduce.5.cloned.1.call-start = ((), (), s32[]{:S(2)}) async-start(), calls=%async_computation.4 | async-start | bytes 786432 | tf_op jit(solution)/shard_map/psum | solution.py:10
  242.9 1.1 copy-start.2
  244.0 1.2 copy-start.1
  244.0 1.2 copy-start.4
  247.4 250.9 %all-reduce.7.cloned.1.call-start = ((), (), s32[]{:S(2)}) async-start(), calls=%async_computation.5 | async-start | bytes 786432 | tf_op jit(solution)/shard_map/psum | solution.py:11
  473.3 30.6 %collective-permute-start.10 = (bf16[]{:T(256)}, bf16[]{:T(256)}, u32[]{:S(2)}, u32[]{:S(2)}) collective-permute-start(bf16[]{:T(256)} %convert_element_type.60), channel_id=1, source_target_pairs={{256,0},{257,1},{258,2},{259,3},{260,4},{261,5},{262,6},{263,7},{2... | collective-permute-start | bytes 14 | tf_op jit(solution)/shard_map/ppermute | solution.py:30
  501.7 3.0 collective-permute-start.9
Sparse Core Ops, SparseCore 0:
  11.7 91.6 all-gather.2
  247.5 150.2 all-reduce.4
  400.2 75.1 all-reduce.6
